TPU v7x, 32 devices: a whole 2x2x4 slice. The times are simulated.
32 devices in a mesh: freq: 4 (over x, core), tile: 8 (over z, y).
Axes of the slice: x: 2, y: 2, z: 4, core: 2. Of those that a mesh axis runs over, the one named last changes fastest.
Arguments:
- plus_time: bfloat16 [128, 128, 12288], P('freq', None, 'tile'), may hold values from -6 to 6
- minus_time: bfloat16 [128, 128, 12288], P('freq', None, 'tile'), may hold values from -6 to 6
- gate_starts: int32 [128, 48], P('freq', 'tile'), may hold values from 0 to 64
- tile_ranks: int32 [4, 48, 48], P('freq', None, 'tile'), may hold values from 1 to 64, as said below
- u_factors: bfloat16 [4, 48, 48, 2, 64, 256], P('freq', 'tile'), may hold values from -0.109375 to 0.109375
- v_factors: bfloat16 [4, 48, 48, 2, 64, 256], P('freq', None, 'tile'), may hold values from -0.375 to 0.375
Outputs:
- minus_new: bfloat16 [4, 2, 128, 12288], P('freq', None, None, 'tile')
- plus_new: bfloat16 [4, 2, 128, 12288], P('freq', None, None, 'tile')
- cross_gram: float32 [4, 2, 128, 128], P('freq', None, 'tile')
- normal_gram: float32 [4, 2, 128, 128], P('freq', None, 'tile')
Inputs may be any that keep to these rules, and one draw needn't show every extreme that they name: `tile_ranks`: tiles with |i - j| <= 1 have rank 64; every other tile has rank at most 32, and some tile of every draw has exactly 32.
All inputs are finite; a program needn't handle non-finite values.
Results may differ from a plain program's by a relative error of at most 0.014.
Values may be sent and summed in bfloat16 or wider, within the bound.
A program may use at most 192 MiB of HBM per device.

v0:
```python
import math

import jax
import jax.numpy as jnp
from jax import lax
from jax.sharding import PartitionSpec as P

R = 12288
GATE = 64


def extended(x, sides, width):
    for axis, dim in sides:
        size, length = (lax.axis_size(axis), x.shape[dim])
        up = [(i, (i + 1) % size) for i in range(size - 1)]
        down = [(j, i) for i, j in up]
        last = lax.slice_in_dim(x, length - width, length, axis=dim)
        leading = lax.slice_in_dim(x, 0, width, axis=dim)
        before = lax.ppermute(last, axis, up)
        after = lax.ppermute(leading, axis, down)
        x = jnp.concatenate([before, x, after], axis=dim)
    return x


def make_table(freq_count, sample_count):
    freq_ids = lax.broadcasted_iota(jnp.int32, (freq_count, sample_count), 0)
    sample_ids = lax.broadcasted_iota(jnp.int32, (freq_count, sample_count), 1)
    phase_ids = freq_ids * sample_ids % sample_count
    angles = phase_ids.astype(jnp.float32) * (2.0 * math.pi / sample_count)
    amplitude = 1.0 / math.sqrt(GATE)
    return jnp.stack([jnp.cos(angles) * amplitude, -jnp.sin(angles) * amplitude]).astype(
        jnp.bfloat16
    )


def half_signs(entry_count):
    entry_ids = lax.broadcasted_iota(jnp.int32, (entry_count,), 0)
    return jnp.where(entry_ids < entry_count // 2, 1.0, -1.0).astype(jnp.float32)


def gate_field(traces, gate_starts):
    sources, samples, receivers = traces.shape
    blocks = gate_starts.shape[1]
    shaped = traces.reshape(sources, samples, blocks, receivers // blocks)
    sample_ids = lax.broadcasted_iota(jnp.int32, (1, samples, 1, 1), 1)
    starts = gate_starts[:, None, :, None]
    inside = (sample_ids >= starts) & (sample_ids < starts + GATE)
    kept = jnp.where(inside, shaped, jnp.zeros((), traces.dtype))
    return kept.reshape(sources, samples, receivers)


def on_device(plus_time, minus_time, gate_starts, tile_ranks, u_factors, v_factors):
    f_local = u_factors.shape[0]
    row_tiles = u_factors.shape[1]
    all_tiles = u_factors.shape[2]
    col_tiles = v_factors.shape[2]
    rank_depth = v_factors.shape[4]
    half_depth = rank_depth // 2
    freq_total = f_local * lax.axis_size("freq")
    sample_count = plus_time.shape[1]
    stacked = jnp.stack([gate_field(plus_time, gate_starts), gate_field(minus_time, gate_starts)])
    dft_table = make_table(freq_total, sample_count)
    local_spec = jnp.einsum(
        "cft,qstr->fcqsr", dft_table, stacked, preferred_element_type=jnp.float32
    ).astype(jnp.bfloat16)
    spectra = lax.all_to_all(local_spec, "freq", split_axis=0, concat_axis=3, tiled=True)
    both_sources = 2 * spectra.shape[3]
    columns = spectra.reshape(f_local, 2, both_sources, col_tiles, spectra.shape[4] // col_tiles)
    sign_vec = half_signs(both_sources)
    partial_c = jnp.einsum(
        "fijckr,fdsjr->fijcdks", v_factors, columns, preferred_element_type=jnp.float32
    )
    coeff_real = partial_c[:, :, :, 0, 0] - sign_vec * partial_c[:, :, :, 1, 1]
    coeff_imag = partial_c[:, :, :, 0, 1] + sign_vec * partial_c[:, :, :, 1, 0]
    rank_ids = lax.broadcasted_iota(jnp.int32, (1, 1, 1, rank_depth), 3)
    rank_mask = (rank_ids < tile_ranks[:, :, :, None]).astype(jnp.float32)[..., None]
    coeff_all = jnp.stack([coeff_real * rank_mask, coeff_imag * rank_mask], 3).astype(jnp.bfloat16)
    lower_part = coeff_all[:, :, :, :, :half_depth]
    lower_rows = lax.all_to_all(lower_part, "tile", split_axis=1, concat_axis=2, tiled=True)
    products = jnp.einsum(
        "fijckr,fijeks->fcesir",
        u_factors[:, :, :, :, :half_depth],
        lower_rows,
        preferred_element_type=jnp.float32,
    )
    block_start = lax.axis_index("tile") * col_tiles
    local_ids = lax.broadcasted_iota(jnp.int32, (col_tiles,), 0)
    global_cols = block_start + local_ids
    band_list = []
    for offset in (-1, 0, 1):
        band_rows = global_cols + offset
        valid = (band_rows >= 0) & (band_rows < all_tiles)
        clipped = jnp.clip(band_rows, 0, all_tiles - 1)
        picked = coeff_all[:, clipped, local_ids][:, :, :, half_depth:]
        band_list.append(
            jnp.where(valid[None, :, None, None, None], picked, jnp.zeros((), picked.dtype))
        )
    band_upper = jnp.stack(band_list, 1)
    padded_band = extended(band_upper, (("tile", 2),), 1)
    row_global = lax.axis_index("tile") * row_tiles + lax.broadcasted_iota(
        jnp.int32, (row_tiles,), 0
    )
    row_local = lax.broadcasted_iota(jnp.int32, (row_tiles,), 0)
    coeff_band = []
    u_band = []
    for position, offset in enumerate((-1, 0, 1)):
        coeff_band.append(padded_band[:, position, 1 - offset : 1 - offset + row_tiles])
        partner = jnp.clip(row_global - offset, 0, all_tiles - 1)
        u_band.append(u_factors[:, row_local, partner][:, :, :, half_depth:])
    band_products = jnp.einsum(
        "fdickr,fdieks->fcesir",
        jnp.stack(u_band, 1),
        jnp.stack(coeff_band, 1),
        preferred_element_type=jnp.float32,
    )
    products = products + band_products
    resp_real = products[:, 0, 0] - sign_vec[:, None, None] * products[:, 1, 1]
    resp_imag = products[:, 0, 1] + sign_vec[:, None, None] * products[:, 1, 0]
    response = jnp.stack([resp_real, resp_imag], 1).reshape(f_local, 2, both_sources, -1)
    rounded = response.astype(jnp.bfloat16)
    half_count = both_sources // 2
    minus_new = rounded[:, :, :half_count]
    plus_new = rounded[:, :, half_count:]
    gram_parts = jnp.einsum(
        "fczr,fesr->fczes", rounded, plus_new, preferred_element_type=jnp.float32
    )
    gram_real = gram_parts[:, 0, :, 0] + gram_parts[:, 1, :, 1]
    gram_imag = gram_parts[:, 1, :, 0] - gram_parts[:, 0, :, 1]
    row_ids = lax.broadcasted_iota(jnp.int32, (both_sources, 1), 0)
    row_scale = jnp.where(row_ids < half_count, 1.0 / math.sqrt(R), 1.0 / R).astype(jnp.float32)
    gram_all = jnp.stack([gram_real * row_scale, gram_imag * row_scale], 1)
    gram_all = gram_all.reshape(f_local, 2, 2, half_count, half_count).transpose(0, 2, 1, 3, 4)
    gram_total = lax.psum(gram_all.astype(jnp.bfloat16), "tile").astype(jnp.float32)
    row_share = half_count // lax.axis_size("tile")
    own_rows = lax.dynamic_slice_in_dim(
        gram_total, lax.axis_index("tile") * row_share, row_share, 3
    )
    return (minus_new, plus_new, own_rows[:, 0], own_rows[:, 1])


def solution(mesh):
    placed = (
        P("freq", None, "tile"),
        P("freq", None, "tile"),
        P("freq", "tile"),
        P("freq", None, "tile"),
        P("freq", "tile", None, None, None, None),
        P("freq", None, "tile", None, None, None),
    )
    return jax.shard_map(
        on_device,
        mesh=mesh,
        in_specs=placed,
        out_specs=(
            P("freq", None, None, "tile"),
            P("freq", None, None, "tile"),
            P("freq", None, "tile", None),
            P("freq", None, "tile", None),
        ),
        check_vma=False,
    )
```

profile of v0, /device:TPU:0, one launch (start us, length us, event | category | flops | bytes accessed | tf_op | source)
XLA Modules:
  0.0 496.3 jit_solution(5784172588843423811)
XLA Ops:
  8.9 4.3 broadcast_in_dim.81
  13.2 14.4 %copy.68 = pred[32,128,1536]{2,1,0:T(8,128)(4,1)} copy(pred[32,128,1536]{1,2,0:T(8,128)(4,1)} %bitcast.187) | data formatting | bytes 12582912 | tf_op jit(solution)/shard_map/jit(_where)/broadcast_in_dim | solution.py:48
  27.6 15.3 %select_bitcast_fusion.1 = (bf16[1,32,128,1536]{3,2,1,0:T(8,128)(2,1)S(1)}, bf16[1,32,128,1536]{3,2,1,0:T(8,128)(2,1)}) fusion(pred[32,128,1536]{2,1,0:T(8,128)(4,1)} %copy.68, bf16[32,128,1536]{2,1,0:T(8,128)(2,1)} %param.6, bf16[32,128,1536]{2,1,0:T(8,128)(2,1)} %param.7), kind=kLoop, calls=%fused_computation.27 | loop fusion | flops 12582912 | bytes 56623104 | tf_op jit(solution)/shard_map/jit(_where)/select_n | solution.py:48
  42.9 6.8 %fusion.18 = bf16[4,2,2,32,1536]{4,0,1,3,2:T(4,128)(2,1)S(1)} fusion(bf16[1,32,128,1536]{3,2,1,0:T(8,128)(2,1)} %get-tuple-element.11, bf16[1,32,128,1536]{3,2,1,0:T(8,128)(2,1)S(1)} %get-tuple-element.10, bf16[1,4,128]{2,1,0:T(4,128)(2,1)S(1)} %get-tuple-element.24, bf16[1,4,128]{2,1,0:T(4,128)(2,1)S(1)} %get-tuple-element.25), kind=kOutput, calls=%fused_computation.37 | convolution fusion | flops 252448768 | bytes 26740736 | tf_op jit(solution)/shard_map/cft,qstr->fcqsr/dot_general | solution.py:63
  52.1 4.2 all-to-all-start
  56.5 19.9 %all-to-all-done = bf16[4,2,2,32,1536]{4,1,3,2,0:T(2,128)(2,1)S(1)} async-done(((bf16[4,2,2,32,1536]{4,1,3,2,0:T(2,128)(2,1)}), bf16[4,2,2,32,1536]{4,1,3,2,0:T(2,128)(2,1)S(1)}, u32[]{:S(2)}, u32[]{:S(2)}) %all-to-all-start) | async-done | bytes 1572896 | tf_op jit(solution)/shard_map/all_to_all | solution.py:66
  81.1 32.4 %convolution_bitcast_fusion = f32[1,48,6,2,2,64,256]{6,5,3,1,4,2,0:T(8,128)} fusion(bf16[2,256,6,256,1,1]{3,2,1,0,5,4:T(8,128)(2,1)S(1)} %bitcast.189, bf16[1,48,6,2,64,256]{5,4,3,2,1,0:T(8,128)(2,1)} %param.11), kind=kOutput, calls=%fused_computation.6 | convolution fusion | flops 9663676416 | bytes 95944704 | tf_op jit(solution)/shard_map/fijckr,fdsjr->fijcdks/dot_general | solution.py:70
  113.5 24.0 %fusion.12 = (bf16[1,48,6,1,64,256]{5,4,1,2,3,0:T(8,128)(2,1)S(1)}, bf16[1,48,6,1,64,256]{5,4,1,2,3,0:T(8,128)(2,1)S(1)}) fusion(f32[1,48,6,2,2,64,256]{6,5,3,1,4,2,0:T(8,128)} %convolution_bitcast_fusion, f32[48,6,64]{2,0,1:T(8,128)S(1)} %fusion.49, f32[256]{0:T(256)S(1)} %compare_select_fusion.4), kind=kLoop, calls=%fused_computation.29 | loop fusion | flops 37748736 | bytes 94446592 | tf_op jit(solution)/shard_map/stack | solution.py:77
  143.9 4.1 fusion.13
  148.0 9.0 %copy.77 = bf16[1,48,6,2,32,256]{5,4,2,3,0,1:T(8,128)(2,1)} copy(bf16[1,48,6,2,32,256]{5,4,1,2,3,0:T(8,128)(2,1)} %fusion.13) | data formatting | bytes 18874368 | tf_op jit(solution)/shard_map/slice | solution.py:78
  157.0 6.6 %all-to-all-start.1 = ((bf16[1,48,6,2,32,256]{5,4,2,3,0,1:T(8,128)(2,1)}), bf16[1,48,6,2,32,256]{5,4,2,3,0,1:T(8,128)(2,1)}, u32[]{:S(2)}, u32[]{:S(2)}) async-start(bf16[1,48,6,2,32,256]{5,4,2,3,0,1:T(8,128)(2,1)} %copy.77), calls=%async_computation.1 | async-start | bytes 18874368 | tf_op jit(solution)/shard_map/all_to_all | solution.py:79
  163.7 6.9 %gather_fusion.5 = bf16[6,2,64,256]{3,2,1,0:T(8,128)(2,1)S(1)} fusion(bf16[6,48,2,64,256]{4,3,2,1,0:T(8,128)(2,1)} %bitcast.205, s32[6]{0:T(128)S(1)} %get-tuple-element.28), kind=kCustom, calls=%fused_computation.5 | custom fusion | bytes 786480 | tf_op jit(solution)/shard_map/gather | solution.py:109
  170.7 6.9 %gather_fusion.4 = bf16[6,2,64,256]{3,2,1,0:T(8,128)(2,1)S(1)} fusion(bf16[6,48,2,64,256]{4,3,2,1,0:T(8,128)(2,1)} %bitcast.206, s32[6]{0:T(128)S(1)} %get-tuple-element.29), kind=kCustom, calls=%fused_computation.4 | custom fusion | bytes 786480 | tf_op jit(solution)/shard_map/gather | solution.py:109
  177.6 6.9 %gather_fusion.3 = bf16[6,2,64,256]{3,2,1,0:T(8,128)(2,1)S(1)} fusion(bf16[6,48,2,64,256]{4,3,2,1,0:T(8,128)(2,1)} %bitcast.207, s32[6]{0:T(128)S(1)} %get-tuple-element.30), kind=kCustom, calls=%fused_computation.3 | custom fusion | bytes 786480 | tf_op jit(solution)/shard_map/gather | solution.py:109
  184.7 16.5 %fusion.1 = bf16[48,6,2,64,256]{4,3,0,1,2:T(8,128)(2,1)} fusion(bf16[1,48,6,1,64,256]{5,4,1,2,3,0:T(8,128)(2,1)} %copy-done, bf16[1,48,6,1,64,256]{5,4,1,2,3,0:T(8,128)(2,1)} %copy-done.1), kind=kLoop, calls=%fused_computation.12 | loop fusion | flops 9437184 | bytes 37748736 | tf_op jit(solution)/shard_map/stack | solution.py:77
  201.2 6.9 %gather_fusion.2 = bf16[6,2,64,256]{3,2,1,0:T(8,128)(2,1)S(1)} fusion(bf16[48,6,2,64,256]{4,3,0,1,2:T(8,128)(2,1)} %fusion.1, s32[6]{0:T(128)S(1)} %get-tuple-element.31), kind=kCustom, calls=%fused_computation.2 | custom fusion | bytes 786480 | tf_op jit(solution)/shard_map/gather | solution.py:94
  208.2 6.9 %gather_fusion.1 = bf16[6,2,64,256]{3,2,1,0:T(8,128)(2,1)S(1)} fusion(bf16[48,6,2,64,256]{4,3,0,1,2:T(8,128)(2,1)} %fusion.1, s32[6]{0:T(128)S(1)} %get-tuple-element.32), kind=kCustom, calls=%fused_computation.1 | custom fusion | bytes 786480 | tf_op jit(solution)/shard_map/gather | solution.py:94
  215.1 6.9 %gather_fusion = bf16[6,2,64,256]{3,2,1,0:T(8,128)(2,1)S(1)} fusion(bf16[48,6,2,64,256]{4,3,0,1,2:T(8,128)(2,1)} %fusion.1, s32[6]{0:T(128)S(1)} %get-tuple-element.33), kind=kCustom, calls=%fused_computation | custom fusion | bytes 786480 | tf_op jit(solution)/shard_map/gather | solution.py:94
  223.8 4.6 collective-permute-start.1
  228.3 141.7 %all-to-all-done.1 = bf16[1,48,6,2,32,256]{5,4,2,3,0,1:T(8,128)(2,1)} async-done(((bf16[1,48,6,2,32,256]{5,4,2,3,0,1:T(8,128)(2,1)}), bf16[1,48,6,2,32,256]{5,4,2,3,0,1:T(8,128)(2,1)}, u32[]{:S(2)}, u32[]{:S(2)}) %all-to-all-start.1) | async-done | bytes 9437216 | tf_op jit(solution)/shard_map/all_to_all | solution.py:79
  370.0 9.1 %copy.78 = bf16[1,48,6,2,32,256]{5,4,3,2,1,0:T(8,128)(2,1)} copy(bf16[1,48,6,2,32,256]{5,4,2,3,0,1:T(8,128)(2,1)} %all-to-all-done.1) | data formatting | bytes 18874368 | tf_op jit(solution)/shard_map/all_to_all | solution.py:79
  379.1 9.5 %copy.79 = bf16[1,6,8,6,2,32,256]{6,5,4,3,2,1,0:T(8,128)(2,1)} copy(bf16[1,6,8,6,2,32,256]{6,5,4,3,1,2,0:T(8,128)(2,1)} %bitcast.186) | data formatting | bytes 18874368 | tf_op jit(solution)/shard_map/all_to_all | solution.py:79
  388.6 12.0 %fusion.14 = f32[6,2,256,2,256,1]{2,4,5,3,1,0:T(8,128)} fusion(bf16[6,48,2,32,256,1]{4,3,2,1,0,5:T(8,128)(2,1)} %bitcast.188, bf16[1,6,48,2,64,256]{5,4,3,2,1,0:T(8,128)(2,1)} %param.10), kind=kOutput, calls=%fused_computation.32 | convolution fusion | flops 4831838208 | bytes 25165824 | tf_op jit(solution)/shard_map/fijckr,fijeks->fcesir/dot_general | solution.py:80
  420.2 68.0 %all-reduce.2.cloned.1.call-done = bf16[1,2,2,128,128]{4,3,2,1,0:T(8,128)(2,1)} async-done(((bf16[1,2,2,128,128]{4,3,2,1,0:T(8,128)(2,1)}), bf16[1,2,2,128,128]{4,3,2,1,0:T(8,128)(2,1)}) %all-reduce.2.cloned.1.call-update) | async-done | bytes 131088 | tf_op jit(solution)/shard_map/psum | solution.py:133
  (52 shorter events, 37.9 us)
Async XLA Ops:
  49.7 6.6 %copy-start.3 = (s32[1,48,6]{1,0,2:T(1,128)S(1)}, s32[1,48,6]{1,0,2:T(1,128)}, u32[]{:S(2)}) copy-start(s32[1,48,6]{1,0,2:T(1,128)} %param.9) | copy-start | bytes 3460
  52.1 24.3 %all-to-all-start = ((bf16[4,2,2,32,1536]{4,1,3,2,0:T(2,128)(2,1)}), bf16[4,2,2,32,1536]{4,1,3,2,0:T(2,128)(2,1)S(1)}, u32[]{:S(2)}, u32[]{:S(2)}) async-start(bf16[4,2,2,32,1536]{4,1,3,2,0:T(2,128)(2,1)} %copy.70), calls=%async_computation | async-start | bytes 3145728 | tf_op jit(solution)/shard_map/all_to_all | solution.py:66
  137.6 3.6 copy-start
  137.6 6.4 %copy-start.1 = (bf16[1,48,6,1,64,256]{5,4,1,2,3,0:T(8,128)(2,1)}, bf16[1,48,6,1,64,256]{5,4,1,2,3,0:T(8,128)(2,1)S(1)}, u32[]{:S(2)}) copy-start(bf16[1,48,6,1,64,256]{5,4,1,2,3,0:T(8,128)(2,1)S(1)} %get-tuple-element.5) | copy-start | bytes 28311556
  157.0 213.0 %all-to-all-start.1 = ((bf16[1,48,6,2,32,256]{5,4,2,3,0,1:T(8,128)(2,1)}), bf16[1,48,6,2,32,256]{5,4,2,3,0,1:T(8,128)(2,1)}, u32[]{:S(2)}, u32[]{:S(2)}) async-start(bf16[1,48,6,2,32,256]{5,4,2,3,0,1:T(8,128)(2,1)} %copy.77), calls=%async_computation.1 | async-start | bytes 18874368 | tf_op jit(solution)/shard_map/all_to_all | solution.py:79
  163.6 324.5 %all-reduce.2.cloned.1.call-start = ((), (), s32[]{:S(2)}) async-start(), calls=%async_computation.2 | async-start | bytes 262144 | tf_op jit(solution)/shard_map/psum | solution.py:133
  222.5 178.2 %collective-permute-start = (bf16[1,3,1,2,32,256]{5,4,3,2,1,0:T(8,128)(2,1)S(1)}, bf16[1,3,1,2,32,256]{5,4,3,2,1,0:T(8,128)(2,1)S(1)}, u32[]{:S(2)}, u32[]{:S(2)}) collective-permute-start(bf16[1,3,1,2,32,256]{5,4,3,2,1,0:T(8,128)(2,1)S(1)} %get-tuple-element.14), channel_id=1, source_target_pairs={{1,0},{2,1},{3,2},{4,3},{5,4},{6,5},{7,6},{9,8},{10,9},{11,10},{12... | collective-permute-start | bytes 294920 | tf_op jit(solution)/shard_map/ppermute | solution.py:20
  223.8 176.9 %collective-permute-start.1 = (bf16[1,3,1,2,32,256]{5,4,3,2,1,0:T(8,128)(2,1)S(1)}, bf16[1,3,1,2,32,256]{5,4,3,2,1,0:T(8,128)(2,1)S(1)}, u32[]{:S(2)}, u32[]{:S(2)}) collective-permute-start(bf16[1,3,1,2,32,256]{5,4,3,2,1,0:T(8,128)(2,1)S(1)} %get-tuple-element.15), channel_id=1, source_target_pairs={{0,1},{1,2},{2,3},{3,4},{4,5},{5,6},{6,7},{8,9},{9,10},{10,11},{11... | collective-permute-start | bytes 294920 | tf_op jit(solution)/shard_map/ppermute | solution.py:19
  418.7 70.7 %copy-start.2 = (bf16[1,2,128,1536]{3,2,1,0:T(8,128)(2,1)}, bf16[1,2,128,1536]{3,2,1,0:T(8,128)(2,1)S(1)}, u32[]{:S(2)}) copy-start(bf16[1,2,128,1536]{3,2,1,0:T(8,128)(2,1)S(1)} %get-tuple-element.12) | copy-start | bytes 2359300
Sparse Core Ops, SparseCore 0:
  420.3 67.7 all-reduce.1
where the time goes:
time: 498 us; the launch traced here: 496 us
  waiting for transfers between devices  230 us (46%)
  local copies, waits for them, and re-layouts  113 us (23%)
  other arithmetic  67 us (13%)
  matrix products  55.3 us (11%)
  starting transfers between devices  16.7 us (3%)
  between operations  14.3 us (3%)
    all_to_all x1, waiting for transfers between devices, on_device(): lax.all_to_all(lower_part, 'tile', split_axis=1, concat_axis=2, tiled=True)  142 us
    psum x1, waiting for transfers between devices, on_device(): lax.psum(gram_all.astype(jnp.bfloat16), 'tile').astype(jnp.float32)  68 us
    another operation x3, other arithmetic, on_device(): jnp.stack([coeff_real * rank_mask, coeff_imag * rank_mask], 3)  44.6 us
    dot_general x1, matrix products, on_device(): jnp.einsum('fijckr,fdsjr->fijcdks', v_factors, columns, preferred_element...  32.4 us
    gather x3, local copies, waits for them, and re-layouts, on_device(): u_band.append(u_factors[:, row_local, partner][:, :, :, half_depth:])  20.8 us
    gather x3, local copies, waits for them, and re-layouts, on_device(): picked = coeff_all[:, clipped, local_ids][:, :, :, half_depth:]  20.8 us
    all_to_all x1, waiting for transfers between devices, on_device(): lax.all_to_all(local_spec, 'freq', split_axis=0, concat_axis=3, tiled=True)  19.9 us
    broadcast_in_dim x2, local copies, waits for them, and re-layouts, gate_field(): kept = jnp.where(inside, shaped, jnp.zeros((), traces.dtype))  18.7 us
  transfers between devices with their start and end apart: 5, of which 3 were waited for; matrix products, arithmetic and copies ran while one was open for 18% of the time, Pallas kernels for 0%

commit v1 on v0

v1 whole, which is shorter than its diff:
```python
import functools
import math

import jax
import jax.numpy as jnp
from jax import lax
from jax.experimental import pallas as pl
from jax.experimental.pallas import tpu as pltpu
from jax.sharding import PartitionSpec as P

GATE = 64
MESH = pl.DeviceIdType.MESH
NT_DIMS = (((1,), (1,)), ((), ()))
TN_DIMS = (((0,), (0,)), ((), ()))


def make_table(freq_count, sample_count):
    freq_ids = lax.broadcasted_iota(jnp.int32, (freq_count, sample_count), 0)
    sample_ids = lax.broadcasted_iota(jnp.int32, (freq_count, sample_count), 1)
    phase_ids = freq_ids * sample_ids % sample_count
    angles = phase_ids.astype(jnp.float32) * (2.0 * math.pi / sample_count)
    amplitude = 1.0 / math.sqrt(GATE)
    return jnp.stack([jnp.cos(angles) * amplitude, -jnp.sin(angles) * amplitude]).astype(
        jnp.bfloat16
    )


def spectra_kernel(starts, table, plus, minus, out):
    block, tile = pl.program_id(0), pl.program_id(1)
    freqs, _, _, sources, width = out.shape
    samples = plus.shape[1]
    shape = (2 * freqs, sources, 2 * samples)
    rows = 2 * freqs * sources
    row_source = lax.broadcasted_iota(jnp.int32, shape, 1).reshape(rows, 2 * samples)
    column = lax.broadcasted_iota(jnp.int32, (rows, 2 * samples), 1)
    second = column >= samples
    sample = jnp.where(second, column - samples, column)
    row_source = row_source - second.astype(jnp.int32)
    values = table[...]
    total_plus = jnp.zeros((rows, width), jnp.float32)
    total_minus = jnp.zeros((rows, width), jnp.float32)
    for pair in range(sources // 2):
        first_id = block * sources + 2 * pair
        start = jnp.where(second, starts[first_id + 1, tile], starts[first_id, tile])
        inside = (sample >= start) & (sample < start + GATE) & (row_source == 2 * pair)
        gated = jnp.where(inside, values, 0.0).astype(jnp.bfloat16)
        both = slice(2 * pair, 2 * pair + 2)
        total_plus += jnp.dot(
            gated, plus[both].reshape(2 * samples, width), preferred_element_type=jnp.float32
        )
        total_minus += jnp.dot(
            gated, minus[both].reshape(2 * samples, width), preferred_element_type=jnp.float32
        )
    out[:, :, 0] = total_plus.reshape(freqs, 2, sources, width).astype(out.dtype)
    out[:, :, 1] = total_minus.reshape(freqs, 2, sources, width).astype(out.dtype)


def local_spectra(plus_time, minus_time, gate_starts, freq_total):
    sources, samples, receivers = plus_time.shape
    tiles = gate_starts.shape[1]
    width = receivers // tiles
    block = math.gcd(16, sources)
    table = make_table(freq_total, samples).transpose(1, 0, 2).astype(jnp.float32)
    table = jnp.broadcast_to(table[:, :, None, None], (freq_total, 2, block, 2, samples))
    table = table.reshape(freq_total * 2 * block, 2 * samples)
    return pl.pallas_call(
        spectra_kernel,
        grid=(sources // block, tiles),
        in_specs=[
            pl.BlockSpec(memory_space=pltpu.SMEM),
            pl.BlockSpec(table.shape, lambda b, j: (0, 0)),
            pl.BlockSpec((block, samples, width), lambda b, j: (b, 0, j)),
            pl.BlockSpec((block, samples, width), lambda b, j: (b, 0, j)),
        ],
        out_specs=pl.BlockSpec((freq_total, 2, 2, block, width), lambda b, j: (0, 0, 0, b, j)),
        out_shape=jax.ShapeDtypeStruct((freq_total, 2, 2, sources, receivers), jnp.bfloat16),
        name="gated_spectra",
    )(gate_starts, table, plus_time, minus_time)


def partner(me, step):
    other, bit = me, 1
    while bit <= step:
        if step & bit:
            other = other + bit - 2 * bit * ((me // bit) % 2)
        bit *= 2
    return other


def swapped(block, count, axis):
    parts = [lax.slice_in_dim(block, n * count, (n + 1) * count, axis=axis) for n in range(4)]
    return jnp.concatenate([-parts[2], parts[3], parts[0], -parts[1]], axis=axis)


def operator_kernel(
    n, nf, ranks, spec, u_hbm, v_hbm, minus, plus, cross, normal,
    xall, v_s, u_s, vb, ub, send, recv, cband, bin_, acc, gsum, gsend, grecv,
    sem_v, sem_u, sem_vb, sem_ub, fsend, frecv, csend, crecv, bsend, brecv, gs_sem, gr_sem,
):
    me = lax.axis_index("tile")
    mf = lax.axis_index("freq")
    tiles, half, width = v_s.shape[0], v_s.shape[3], v_s.shape[4]
    sl = spec.shape[3]
    count = sl * nf
    lanes = 4 * count
    base = me * tiles
    total_tiles = n * tiles
    first = 1 - (me + n - 1) // n
    last = (me + 1) // n

    def load_v(j):
        return pltpu.make_async_copy(
            v_hbm.at[0, :, j, :, pl.ds(0, half), :], v_s.at[j], sem_v.at[j]
        )

    def load_u(m):
        src = partner(me, m)
        return pltpu.make_async_copy(
            u_hbm.at[0, :, pl.ds(src * tiles, tiles), :, pl.ds(0, half), :], u_s.at[m], sem_u.at[m]
        )

    def load_band(o, j, right):
        row, col = base + j + o - 1, base + j - o + 1
        if j + o - 1 < 0:
            row = row + first
        if j + o - 1 >= tiles:
            row = row - last
        if j - o + 1 < 0:
            col = col + first
        if j - o + 1 >= tiles:
            col = col - last
        if right:
            return pltpu.make_async_copy(
                v_hbm.at[0, row, j, :, pl.ds(half, half), :], vb.at[o, j], sem_vb.at[o, j]
            )
        return pltpu.make_async_copy(
            u_hbm.at[0, j, col, :, pl.ds(half, half), :], ub.at[o, j], sem_ub.at[o, j]
        )

    def columns(j):
        return pl.ds(pl.multiple_of(j * width, width), width)

    def freq_copy(g, j):
        peer = partner(mf, g)
        return pltpu.make_async_remote_copy(
            src_ref=spec.at[peer, :, :, :, columns(j)],
            dst_ref=xall.at[:, :, pl.ds(pl.multiple_of(mf * sl, sl), sl), columns(j)],
            send_sem=fsend.at[g, j],
            recv_sem=frecv.at[g, j],
            device_id={"freq": peer},
            device_id_type=MESH,
        )

    def coeff_copy(m, j):
        return pltpu.make_async_remote_copy(
            src_ref=send.at[j, m],
            dst_ref=recv.at[j, m],
            send_sem=csend.at[m, j],
            recv_sem=crecv.at[m, j],
            device_id={"tile": partner(me, m)},
            device_id_type=MESH,
        )

    def band_copy(side):
        source = cband.at[2, tiles + 1] if side == 0 else cband.at[0, 0]
        target = lax.rem(me + 1, n) if side == 0 else lax.rem(me + n - 1, n)
        return pltpu.make_async_remote_copy(
            src_ref=source,
            dst_ref=bin_.at[side],
            send_sem=bsend.at[side],
            recv_sem=brecv.at[side],
            device_id={"tile": target},
            device_id_type=MESH,
        )

    def gram_copy(m):
        other = partner(me, m)
        return pltpu.make_async_remote_copy(
            src_ref=gsend.at[other],
            dst_ref=grecv.at[m],
            send_sem=gs_sem.at[m],
            recv_sem=gr_sem.at[m],
            device_id={"tile": other},
            device_id_type=MESH,
        )

    for j in range(tiles):
        load_v(j).start()
        for o in range(3):
            load_band(o, j, True).start()
            load_band(o, j, False).start()
    for m in range(n):
        load_u(m).start()

    barrier = pltpu.get_barrier_semaphore()
    for m in range(1, n):
        pl.semaphore_signal(
            barrier, inc=1, device_id={"tile": partner(me, m)}, device_id_type=MESH
        )
    for g in range(1, nf):
        pl.semaphore_signal(
            barrier, inc=1, device_id={"freq": partner(mf, g)}, device_id_type=MESH
        )
    pl.semaphore_wait(barrier, n + nf - 2)

    for j in range(tiles):
        for g in range(1, nf):
            freq_copy(g, j).start()
    xall[:, :, pl.ds(pl.multiple_of(mf * sl, sl), sl), :] = spec[mf]
    acc[...] = jnp.zeros_like(acc)
    for j in range(tiles):
        for o in range(3):
            load_band(o, j, True).wait()

    rank_id = lax.broadcasted_iota(jnp.int32, (half, lanes), 0)

    def product(a_real, a_imag, b_one, b_two):
        return lax.dot_general(
            a_real, b_one, NT_DIMS, preferred_element_type=jnp.float32
        ) + lax.dot_general(a_imag, b_two, NT_DIMS, preferred_element_type=jnp.float32)

    def coefficients(j, _):
        for g in range(1, nf):
            freq_copy(g, j).wait_recv()
        load_v(j).wait()
        b_one = xall[:, :, :, columns(j)].reshape(lanes, width)
        b_two = swapped(b_one, count, 0)
        for m in list(range(1, n)) + [0]:
            row = partner(me, m) * tiles
            c = product(
                v_s[j, pl.ds(row, tiles), 0].reshape(tiles * half, width),
                v_s[j, pl.ds(row, tiles), 1].reshape(tiles * half, width),
                b_one,
                b_two,
            )
            target = send if m else recv
            for i in range(tiles):
                kept = jnp.where(
                    rank_id < ranks[0, row + i, j], c[i * half : (i + 1) * half], 0.0
                )
                target[j, m, i] = kept.astype(jnp.bfloat16)
            if m:
                coeff_copy(m, j).start()
        c = product(
            vb[:, j, 0].reshape(3 * half, width), vb[:, j, 1].reshape(3 * half, width), b_one, b_two
        ).astype(jnp.bfloat16)
        for o in range(3):
            cband[o, j + o] = c[o * half : (o + 1) * half]
        return 0

    lax.fori_loop(0, tiles, coefficients, 0)
    band_copy(0).start()
    band_copy(1).start()
    for m in range(n):
        load_u(m).wait()
    for j in range(tiles):
        for o in range(3):
            load_band(o, j, False).wait()

    def add(i, c, u_real, u_imag):
        acc[i] += lax.dot_general(
            c, u_real, TN_DIMS, preferred_element_type=jnp.float32
        ) + lax.dot_general(
            swapped(c, count, 1), u_imag, TN_DIMS, preferred_element_type=jnp.float32
        )

    def responses(j, _):
        for m in range(1, n):
            coeff_copy(m, j).wait_recv()

        def one_row(i, _):
            add(
                i,
                recv[j, :, i].reshape(n * half, lanes),
                u_s[:, i, j, 0].reshape(n * half, width),
                u_s[:, i, j, 1].reshape(n * half, width),
            )
            return 0

        return lax.fori_loop(0, tiles, one_row, 0)

    lax.fori_loop(0, tiles - 1, responses, 0)
    band_copy(0).wait_recv()
    band_copy(1).wait_recv()
    zero = jnp.zeros((half, lanes), jnp.bfloat16)
    from_before = jnp.where(first == 0, bin_[0], zero)
    from_after = jnp.where(last == 0, bin_[1], zero)
    for i in range(tiles):
        c = [cband[o, i + 1] for o in range(3)]
        if i == 0:
            c[2] = from_before
        if i == tiles - 1:
            c[0] = from_after
        add(
            i,
            jnp.concatenate(c, axis=0),
            ub[:, i, 0].reshape(3 * half, width),
            ub[:, i, 1].reshape(3 * half, width),
        )
    responses(tiles - 1, 0)

    gsum[...] = jnp.zeros_like(gsum)

    def finish(i, _):
        rounded = acc[i].astype(jnp.bfloat16)
        parts = [rounded[p * count : (p + 1) * count] for p in range(4)]
        for c in range(2):
            minus[0, c, :, columns(i)] = parts[2 * c]
            plus[0, c, :, columns(i)] = parts[2 * c + 1]
        gsum[...] += lax.dot_general(
            rounded,
            jnp.concatenate([parts[1], parts[3]], axis=0),
            NT_DIMS,
            preferred_element_type=jnp.float32,
        )
        return 0

    lax.fori_loop(0, tiles, finish, 0)
    receivers = total_tiles * width
    share = count // n
    for q, scale in enumerate((1.0 / math.sqrt(receivers), 1.0 / receivers)):
        top = slice(q * count, (q + 1) * count)
        low = slice((2 + q) * count, (3 + q) * count)
        real = (gsum[top, :count] + gsum[low, count:]) * scale
        imag = (gsum[low, :count] - gsum[top, count:]) * scale
        for d in range(n):
            gsend[d, q, 0] = real[d * share : (d + 1) * share]
            gsend[d, q, 1] = imag[d * share : (d + 1) * share]
    for m in range(1, n):
        gram_copy(m).start()
    total = gsend[me]
    for m in range(1, n):
        gram_copy(m).wait_recv()
        total = total + grecv[m]
    cross[0] = total[0]
    normal[0] = total[1]

    for j in range(tiles):
        for g in range(1, nf):
            freq_copy(g, j).wait_send()
        for m in range(1, n):
            coeff_copy(m, j).wait_send()
    band_copy(0).wait_send()
    band_copy(1).wait_send()
    for m in range(1, n):
        gram_copy(m).wait_send()


def on_device(n, nf, plus_time, minus_time, gate_starts, tile_ranks, u_factors, v_factors):
    freq_total = u_factors.shape[0] * nf
    tiles = v_factors.shape[2]
    half = v_factors.shape[4] // 2
    width = v_factors.shape[5]
    spec = local_spectra(plus_time, minus_time, gate_starts, freq_total)
    sl, receivers = spec.shape[3], spec.shape[4]
    count = sl * nf
    lanes = 4 * count
    share = count // n
    bf16, f32 = jnp.bfloat16, jnp.float32
    vmem = pl.BlockSpec(memory_space=pltpu.VMEM)
    dma = pltpu.SemaphoreType.DMA
    return pl.pallas_call(
        functools.partial(operator_kernel, n, nf),
        out_shape=(
            jax.ShapeDtypeStruct((1, 2, count, receivers), bf16),
            jax.ShapeDtypeStruct((1, 2, count, receivers), bf16),
            jax.ShapeDtypeStruct((1, 2, share, count), f32),
            jax.ShapeDtypeStruct((1, 2, share, count), f32),
        ),
        in_specs=[
            pl.BlockSpec(memory_space=pltpu.SMEM),
            vmem,
            pl.BlockSpec(memory_space=pl.ANY),
            pl.BlockSpec(memory_space=pl.ANY),
        ],
        out_specs=(vmem, vmem, vmem, vmem),
        scratch_shapes=[
            pltpu.VMEM((2, 2, count, receivers), bf16),
            pltpu.VMEM((tiles, n * tiles, 2, half, width), bf16),
            pltpu.VMEM((n, tiles, tiles, 2, half, width), bf16),
            pltpu.VMEM((3, tiles, 2, half, width), bf16),
            pltpu.VMEM((3, tiles, 2, half, width), bf16),
            pltpu.VMEM((tiles, n, tiles, half, lanes), bf16),
            pltpu.VMEM((tiles, n, tiles, half, lanes), bf16),
            pltpu.VMEM((3, tiles + 2, half, lanes), bf16),
            pltpu.VMEM((2, half, lanes), bf16),
            pltpu.VMEM((tiles, lanes, width), f32),
            pltpu.VMEM((lanes, 2 * count), f32),
            pltpu.VMEM((n, 2, 2, share, count), f32),
            pltpu.VMEM((n, 2, 2, share, count), f32),
            dma((tiles,)),
            dma((n,)),
            dma((3, tiles)),
            dma((3, tiles)),
            dma((nf, tiles)),
            dma((nf, tiles)),
            dma((n, tiles)),
            dma((n, tiles)),
            dma((2,)),
            dma((2,)),
            dma((n,)),
            dma((n,)),
        ],
        compiler_params=pltpu.CompilerParams(
            collective_id=0, has_side_effects=True, vmem_limit_bytes=60 << 20
        ),
        name="reflection_operator",
    )(tile_ranks, spec, u_factors, v_factors)


def solution(mesh):
    placed = (
        P("freq", None, "tile"),
        P("freq", None, "tile"),
        P("freq", "tile"),
        P("freq", None, "tile"),
        P("freq", "tile", None, None, None, None),
        P("freq", None, "tile", None, None, None),
    )
    return jax.shard_map(
        functools.partial(on_device, mesh.shape["tile"], mesh.shape["freq"]),
        mesh=mesh,
        in_specs=placed,
        out_specs=(
            P("freq", None, None, "tile"),
            P("freq", None, None, "tile"),
            P("freq", None, "tile", None),
            P("freq", None, "tile", None),
        ),
        check_vma=False,
    )
```

time: 498 us -> 265 us (0.53)
  Pallas kernels: 0 us -> 253 us
  waiting for transfers between devices: 230 us -> 0 us
  local copies, waits for them, and re-layouts: 113 us -> 10.2 us
  other arithmetic: 67 us -> 0.07 us
  matrix products: 55.3 us -> 0 us
  starting transfers between devices: 16.7 us -> 0 us
  between operations: 14.3 us -> 0.66 us
    pallas_call x0 -> x2, Pallas kernels: none -> 253 us  [the longest x1 239 us: on_device(): pl.pallas_call(functools.partial(operator_kernel, n, nf), out_shape=(jax....]
    all_to_all x2 -> x0, waiting for transfers between devices: 162 us -> none  [the longest x1 142 us: on_device(): lax.all_to_all(lower_part, 'tile', split_axis=1, concat_axis=2, tiled=True)]
    psum x1 -> x0, waiting for transfers between devices: 68 us -> none  [on_device(): lax.psum(gram_all.astype(jnp.bfloat16), 'tile').astype(jnp.float32)]
    dot_general x5 -> x0, matrix products: 55.3 us -> none  [the longest x1 32.4 us: on_device(): jnp.einsum('fijckr,fdsjr->fijcdks', v_factors, columns, preferred_element...]
    another operation x11 -> x1, other arithmetic: 49.3 us -> 0.05 us  [the longest x3 44.6 us: on_device(): jnp.stack([coeff_real * rank_mask, coeff_imag * rank_mask], 3)]
    gather x6 -> x0, local copies, waits for them, and re-layouts: 41.7 us -> none  [the longest x3 20.8 us: on_device(): u_band.append(u_factors[:, row_local, partner][:, :, :, half_depth:])]
    all_to_all x3 -> x0, local copies, waits for them, and re-layouts: 20 us -> none  [the longest x2 18.6 us: on_device(): lax.all_to_all(lower_part, 'tile', split_axis=1, concat_axis=2, tiled=True)]
    broadcast_in_dim x2 -> x1, local copies, waits for them, and re-layouts: 18.7 us -> 0.04 us  [local_spectra(): jnp.broadcast_to(table[:, :, None, None], (freq_total, 2, block, 2, sampl...]
  transfers between devices with their start and end apart: 5 -> 0, of which waited for: 3 -> 0; matrix products, arithmetic and copies ran while one was open for 18% -> 0% of each run, Pallas kernels for 0% -> 0%
where the time goes in v1:
time: 265 us; the launch traced here: 264 us
  Pallas kernels  253 us (95%)
  local copies, waits for them, and re-layouts  10.2 us (4%)
    pallas_call x1, Pallas kernels, on_device(): pl.pallas_call(functools.partial(operator_kernel, n, nf), out_shape=(jax....  239 us
    pallas_call x1, Pallas kernels, local_spectra(): pl.pallas_call(spectra_kernel, grid=(sources // block, tiles), in_specs=[...  14.5 us
    unnamed x7, local copies, waits for them, and re-layouts  10.2 us

profile of v1, /device:TPU:0, one launch (start us, length us, event | category | flops | bytes accessed | tf_op | source)
XLA Modules:
  0.0 264.1 jit_solution(5635580812332839573)
XLA Ops:
  0.6 0.1 multiply_convert_fusion
  0.7 1.4 copy.13.starts
  2.1 1.4 copy.14.ranks
  3.5 0.7 copy.17
  4.2 14.5 %gated_spectra.1.spec = bf16[4,2,2,32,1536]{4,3,2,1,0:T(8,128)(2,1)} custom-call(s32[32,6]{1,0:T(8,128)} %copy.13.starts, f32[128,256]{1,0:T(8,128)} %bitcast.7, bf16[32,128,1536]{2,1,0:T(8,128)(2,1)} %plus.1, bf16[32,128,1536]{2,1,0:T(8,128)(2,1)} %minus.1), custom_call_target="tpu_custom_call" | custom-call | tf_op jit(solution)/shard_map/gated_spectra/pallas_call | solution.py:66
  18.7 238.6 %reflection_operator.1 = (bf16[1,2,128,1536]{3,2,1,0:T(8,128)(2,1)}, bf16[1,2,128,1536]{3,2,1,0:T(8,128)(2,1)}, f32[1,2,16,128]{3,2,1,0:T(8,128)}, f32[1,2,16,128]{3,2,1,0:T(8,128)}) custom-call(s32[1,48,6]{2,1,0:T(8,128)} %copy.14.ranks, bf16[4,2,2,32,1536]{4,3,2,1,0:T(8,128)(2,1)} %gated_spectra.1.spec, bf16[1,6,48,2,64,256]{5,4,3,2,1,0:T(8,128)(2,1)} %u_hbm.1, ...), custom_call_target="tpu_custom_call" | custom-call | tf_op jit(solution)/shard_map/reflection_operator/pallas_call | solution.py:362
  257.3 2.1 copy.22
  259.3 2.1 copy.23
  261.4 1.3 copy.24
  262.7 1.3 copy.25
  (3 shorter events, 0.1 us)

commit v2 on v1

--- a/solution.py
+++ b/solution.py
@@ -107,6 +107,7 @@
     total_tiles = n * tiles
     first = 1 - (me + n - 1) // n
     last = (me + 1) // n
+    inner = ((me + n // 4) // (n // 2)) % 2
 
     def load_v(j):
         return pltpu.make_async_copy(
@@ -239,8 +240,14 @@
                     rank_id < ranks[0, row + i, j], c[i * half : (i + 1) * half], 0.0
                 )
                 target[j, m, i] = kept.astype(jnp.bfloat16)
-            if m:
+            if 0 < m < n // 2:
                 coeff_copy(m, j).start()
+            elif m:
+
+                @pl.when(inner == 1)
+                def _():
+                    coeff_copy(m, j).start()
+
         c = product(
             vb[:, j, 0].reshape(3 * half, width), vb[:, j, 1].reshape(3 * half, width), b_one, b_two
         ).astype(jnp.bfloat16)
@@ -249,6 +256,13 @@
         return 0
 
     lax.fori_loop(0, tiles, coefficients, 0)
+
+    @pl.when(inner == 0)
+    def _():
+        for j in range(tiles):
+            for m in range(n // 2, n):
+                coeff_copy(m, j).start()
+
     band_copy(0).start()
     band_copy(1).start()
     for m in range(n):

time: 265 us -> 265 us (level)
  no operation moved by 1% of the time
where the time goes in v2:
time: 265 us; the launch traced here: 264 us
  Pallas kernels  253 us (95%)
  local copies, waits for them, and re-layouts  10.2 us (4%)
    pallas_call x1, Pallas kernels, on_device(): pl.pallas_call(functools.partial(operator_kernel, n, nf), out_shape=(jax....  239 us
    pallas_call x1, Pallas kernels, local_spectra(): pl.pallas_call(spectra_kernel, grid=(sources // block, tiles), in_specs=[...  14.5 us
    unnamed x7, local copies, waits for them, and re-layouts  10.2 us

profile of v2, /device:TPU:0, one launch (start us, length us, event | category | flops | bytes accessed | tf_op | source)
XLA Modules:
  0.0 264.0 jit_solution(6908852044139220006)
XLA Ops:
  0.6 0.1 multiply_convert_fusion
  0.7 1.4 copy.13.starts
  2.1 1.4 copy.14.ranks
  3.5 0.7 copy.17
  4.2 14.5 %gated_spectra.1.spec = bf16[4,2,2,32,1536]{4,3,2,1,0:T(8,128)(2,1)} custom-call(s32[32,6]{1,0:T(8,128)} %copy.13.starts, f32[128,256]{1,0:T(8,128)} %bitcast.7, bf16[32,128,1536]{2,1,0:T(8,128)(2,1)} %plus.1, bf16[32,128,1536]{2,1,0:T(8,128)(2,1)} %minus.1), custom_call_target="tpu_custom_call" | custom-call | tf_op jit(solution)/shard_map/gated_spectra/pallas_call | solution.py:66
  18.7 238.6 %reflection_operator.1 = (bf16[1,2,128,1536]{3,2,1,0:T(8,128)(2,1)}, bf16[1,2,128,1536]{3,2,1,0:T(8,128)(2,1)}, f32[1,2,16,128]{3,2,1,0:T(8,128)}, f32[1,2,16,128]{3,2,1,0:T(8,128)}) custom-call(s32[1,48,6]{2,1,0:T(8,128)} %copy.14.ranks, bf16[4,2,2,32,1536]{4,3,2,1,0:T(8,128)(2,1)} %gated_spectra.1.spec, bf16[1,6,48,2,64,256]{5,4,3,2,1,0:T(8,128)(2,1)} %u_hbm.1, ...), custom_call_target="tpu_custom_call" | custom-call | tf_op jit(solution)/shard_map/reflection_operator/pallas_call | solution.py:376
  257.3 2.1 copy.22
  259.3 2.1 copy.23
  261.4 1.3 copy.24
  262.7 1.3 copy.25
  (3 shorter events, 0.1 us)
